TPU v7x, 256 devices: a whole 4x4x8 slice. The times are simulated.
256 devices in a mesh: fibre: 2 (over core), chan: 128 (over z, x, y).
Axes of the slice: x: 4, y: 4, z: 8, core: 2. Of those that a mesh axis runs over, the one named last changes fastest.
Arguments:
- raw: bfloat16 [32768, 4096], P(('fibre', 'chan'))
- starts: int32 [4], replicated, may hold values from 0 to 3072, as said below
- ref_ids: int32 [64], replicated, may hold values from 0 to 32767, as said below
- near_ids: int32 [32768, 8], P(('fibre', 'chan')), may hold values from 0 to 32767, as said below
- cross_ids: int32 [32768, 2], P(('fibre', 'chan')), may hold values from 0 to 255
- cross_mask: int32 [32768, 2], P(('fibre', 'chan')), may hold values 0 or 1
- export_loc: int32 [256], P(('fibre', 'chan')), may hold values from 0 to 127
Outputs:
- correlations: bfloat16 [32768, 64, 512], P(('fibre', 'chan'))
Inputs may be any that keep to these rules, and one draw needn't show every extreme that they name: starts[3] is 3072. `ref_ids`: distinct channel ids. `near_ids`: each neighbour lies on the same route as its channel (route = id // 16384) and at most 16 channels away from it.
All inputs are finite; a program needn't handle non-finite values. No bound on the sum of `cross_mask` on one device may be relied on, other than what follows from the above.
Results may differ from a plain program's by a relative error of at most 0.0063.
The roundings to bfloat16 on the way count: a program that leaves them out, or rounds other values in their place, can miss the bound.
Values may be sent and summed in bfloat16 or wider, within the bound.
A program may use at most 128 MiB of HBM per device.

v0:
```python
import math
import jax
import jax.numpy as jnp
from jax import lax
from jax.sharding import PartitionSpec as P

SEG = 1024
SEGS = 4
REFS = 64
LAGS = 512
NN = 8
HALO = 16


def with_halo(block, sides, width):
    for axis, dim in sides:
        count = lax.axis_size(axis)
        forward = [(i, i + 1) for i in range(count - 1)]
        backward = [(target, source) for source, target in forward]
        low = lax.ppermute(
            lax.slice_in_dim(block, block.shape[dim] - width, None, axis=dim), axis, forward
        )
        high = lax.ppermute(lax.slice_in_dim(block, 0, width, axis=dim), axis, backward)
        block = jnp.concatenate([low, block, high], axis=dim)
    return block


def forward_table():
    nbins = SEG // 2
    sample = jnp.arange(SEG, dtype=jnp.int32)
    freq = jnp.arange(nbins, dtype=jnp.int32)
    phase = jnp.mod(sample[:, None] * freq[None, :], SEG).astype(jnp.float32)
    theta = phase * (2.0 * math.pi / SEG)
    keep = (freq > 0).astype(jnp.float32)[None, :]
    return jnp.concatenate([jnp.cos(theta) * keep, -jnp.sin(theta)], 1).astype(jnp.bfloat16)


def lag_table():
    nbins = SEG // 2
    freq = jnp.arange(nbins, dtype=jnp.int32)
    lag = jnp.arange(LAGS, dtype=jnp.int32) - LAGS // 2
    phase = jnp.mod(freq[:, None] * lag[None, :], SEG).astype(jnp.float32)
    theta = phase * (2.0 * math.pi / SEG)
    scale = 1.0 / math.sqrt(nbins)
    table = jnp.concatenate([jnp.cos(theta) * scale, -jnp.sin(theta) * scale], 0)
    return table.astype(jnp.bfloat16)


def per_device(raw, starts, ref_ids, near_ids, cross_ids, cross_mask, export_loc):
    nbins = SEG // 2
    width = SEGS * SEG
    local_ch = raw.shape[0]
    block_base = lax.axis_index(("fibre", "chan")) * local_ch
    pieces = [lax.dynamic_slice_in_dim(raw, starts[s], SEG, 1) for s in range(SEGS)]
    segment = jnp.stack(pieces, 1)
    spectrum = jnp.dot(
        segment.reshape(local_ch * SEGS, SEG), forward_table(), preferred_element_type=jnp.float32
    )
    power = jnp.sum(spectrum * spectrum, -1, keepdims=True) / nbins
    whitened = (spectrum / jnp.sqrt(power + 1e-06)).astype(jnp.bfloat16)
    flat = whitened.reshape(local_ch, width)
    columns = jnp.arange(local_ch, dtype=jnp.int32)
    pick = (ref_ids[:, None] - block_base == columns[None, :]).astype(jnp.bfloat16)
    selected = jnp.dot(pick, flat, preferred_element_type=jnp.float32)
    references = lax.psum(selected, ("fibre", "chan")).astype(jnp.bfloat16)
    extended = with_halo(flat, (("chan", 0),), HALO)
    ext_rows = local_ch + 2 * HALO
    position = near_ids - (block_base - HALO)
    near_count = jnp.sum(
        (position[:, :, None] == jnp.arange(ext_rows, dtype=jnp.int32)[None, None, :]).astype(
            jnp.float32
        ),
        1,
    )
    total = flat.astype(jnp.float32) + jnp.dot(
        near_count.astype(jnp.bfloat16), extended, preferred_element_type=jnp.float32
    )
    exported = jnp.take(flat, export_loc, axis=0)
    live = cross_mask == 1
    piece = lax.all_gather(exported, ("fibre", "chan"), axis=0, tiled=True)
    slots = jnp.arange(piece.shape[0], dtype=jnp.int32)
    hits = (cross_ids[:, :, None] == slots[None, None, :]) & live[:, :, None]
    weights = jnp.sum(hits.astype(jnp.float32), 1).astype(jnp.bfloat16)
    crossing = jnp.dot(weights, piece, preferred_element_type=jnp.float32)
    count = 1.0 + NN + jnp.sum(cross_mask.astype(jnp.float32), 1)
    smoothed = ((total + crossing) / count[:, None]).astype(jnp.bfloat16)
    kernel = lag_table()
    ref_split = references.reshape(REFS, SEGS, SEG)
    ref_re = ref_split[..., :nbins]
    ref_im = ref_split[..., nbins:]
    group = math.gcd(local_ch, 32)

    def correlate(rows):
        a_re = rows[..., :nbins]
        a_im = rows[..., nbins:]
        g_re = jnp.einsum(
            "csf,rsf->crf", a_re, ref_re, preferred_element_type=jnp.float32
        ) + jnp.einsum("csf,rsf->crf", a_im, ref_im, preferred_element_type=jnp.float32)
        g_im = jnp.einsum(
            "csf,rsf->crf", a_im, ref_re, preferred_element_type=jnp.float32
        ) - jnp.einsum("csf,rsf->crf", a_re, ref_im, preferred_element_type=jnp.float32)
        cross = (jnp.concatenate([g_re, g_im], -1) / SEGS).astype(jnp.bfloat16)
        out = jnp.dot(cross.reshape(group * REFS, SEG), kernel, preferred_element_type=jnp.float32)
        return out.astype(jnp.bfloat16).reshape(group, REFS, LAGS)

    result = lax.map(correlate, smoothed.reshape(local_ch // group, group, SEGS, SEG))
    return result.reshape(local_ch, REFS, LAGS)


def solution(mesh):
    in_specs = (
        P(("fibre", "chan"), None),
        P(),
        P(),
        P(("fibre", "chan"), None),
        P(("fibre", "chan"), None),
        P(("fibre", "chan"), None),
        P(("fibre", "chan")),
    )
    out_specs = P(("fibre", "chan"), None, None)
    return jax.shard_map(
        per_device, mesh=mesh, in_specs=in_specs, out_specs=out_specs, check_vma=False
    )
```

profile of v0, /device:TPU:1, one launch (start us, length us, event | category | flops | bytes accessed | tf_op | source)
XLA Modules:
  0.0 315.5 jit_solution(655089644088672558)
XLA Ops:
  13.1 8.0 %negate_convert_fusion = bf16[1024,512]{1,0:T(8,128)(2,1)S(1)} fusion(), kind=kLoop, calls=%fused_computation.36 | loop fusion | flops 8388608 | bytes 1048576 | tf_op jit(solution)/shard_map/convert.3
  26.7 7.9 %multiply_convert_fusion = bf16[1024,512]{1,0:T(8,128)(2,1)S(1)} fusion(f32[512]{0:T(512)S(1)} %fusion.48), kind=kLoop, calls=%fused_computation.37 | loop fusion | flops 8388608 | bytes 1050624 | tf_op jit(solution)/shard_map/convert.2
  44.3 88.9 %all-reduce.1 = bf16[64,4096]{1,0:T(8,128)(2,1)S(1)} all-reduce(f32[64,4096]{1,0:T(8,128)S(1)} %fusion.45), channel_id=1, replica_groups=mesh['fibre'=2,'chan'=128] {'fibre','chan'}, use_global_device_ids=true, to_apply=%region_4.5 | all-reduce | flops 262144 | bytes 1572864 | tf_op jit(solution)/shard_map/psum | solution.py:65
  141.9 16.6 %all-gather.3.cloned.1.call-done = bf16[256,1,4096]{2,1,0:T(2,128)(2,1)} async-done(((bf16[1,1,4096]{2,1,0:T(2,128)(2,1)}), bf16[256,1,4096]{2,1,0:T(2,128)(2,1)}) %all-gather.3.cloned.1.call-update) | async-done | bytes 2097168 | tf_op jit(solution)/shard_map/all_gather | solution.py:80
  164.9 143.8 %while.11 = (s32[]{:T(128)}, bf16[4,32,64,512]{3,2,1,0:T(8,128)(2,1)}, bf16[4,32,4,1024]{3,2,1,0:T(4,128)(2,1)S(1)}, bf16[64,4,512]{0,1,2:T(4,128)(2,1)S(1)}, bf...) while((s32[]{:T(128)}, ...), condition=%wide.region_6.7_spmd, body=%wide.region_5.6_spmd.sunk | while | flops 2190475264 | bytes 77595424 | solution.py:106
  168.1 4.9 %add_bitcast_fusion.2 = f32[32,64,512]{1,0,2:T(8,128)} fusion(f32[512,32,64]{2,1,0:T(8,128)S(1)} %fusion.87, bf16[64,4,512]{0,1,2:T(4,128)(2,1)S(1)} %copy-done.6, bf16[1,32,4,1024]{1,2,3,0:T(4,128)(2,1)S(1)} %copy.57), kind=kOutput, calls=%fused_computation.3.clone.1 | convolution fusion | flops 9437184 | bytes 8912896 | tf_op jit(solution)/shard_map/while/body/eval_jaxpr/csf,rsf->crf/dot_general | solution.py:98
  173.1 6.9 %copy.59 = f32[32,64,512]{2,1,0:T(8,128)} copy(f32[32,64,512]{1,0,2:T(8,128)} %add_bitcast_fusion.2) | data formatting | bytes 8388608 | tf_op jit(solution)/shard_map/while/body/eval_jaxpr/add | solution.py:96
  181.3 4.9 %subtract_bitcast_fusion.2 = f32[32,64,512]{1,0,2:T(8,128)} fusion(f32[512,32,64]{2,1,0:T(8,128)S(1)} %fusion.86, bf16[64,4,512]{0,1,2:T(4,128)(2,1)S(1)} %copy-done.7, bf16[1,32,4,1024]{1,2,3,0:T(4,128)(2,1)S(1)} %copy.57), kind=kOutput, calls=%fused_computation.2.clone.1 | convolution fusion | flops 9437184 | bytes 8912896 | tf_op jit(solution)/shard_map/while/body/eval_jaxpr/csf,rsf->crf/dot_general | solution.py:101
  186.2 6.9 %copy.58 = f32[32,64,512]{2,1,0:T(8,128)} copy(f32[32,64,512]{1,0,2:T(8,128)} %subtract_bitcast_fusion.2) | data formatting | bytes 8388608 | tf_op jit(solution)/shard_map/while/body/eval_jaxpr/sub | solution.py:99
  193.2 5.8 %fusion.88 = bf16[2048,512]{1,0:T(8,128)(2,1)S(1)} fusion(bf16[1024,512]{1,0:T(8,128)(2,1)S(1)} %copy-done.2, f32[2048,512]{1,0:T(8,128)} %bitcast.74, f32[2048,512]{1,0:T(8,128)} %bitcast.73), kind=kOutput, calls=%fused_computation.6.clone.1 | convolution fusion | flops 2154823680 | bytes 11534336 | tf_op jit(solution)/shard_map/while/body/eval_jaxpr/dot_general | solution.py:103
  204.1 4.9 %add_bitcast_fusion.2 = f32[32,64,512]{1,0,2:T(8,128)} fusion(f32[512,32,64]{2,1,0:T(8,128)S(1)} %fusion.87, bf16[64,4,512]{0,1,2:T(4,128)(2,1)S(1)} %copy-done.6, bf16[1,32,4,1024]{1,2,3,0:T(4,128)(2,1)S(1)} %copy.57), kind=kOutput, calls=%fused_computation.3.clone.1 | convolution fusion | flops 9437184 | bytes 8912896 | tf_op jit(solution)/shard_map/while/body/eval_jaxpr/csf,rsf->crf/dot_general | solution.py:98
  209.0 6.9 %copy.59 = f32[32,64,512]{2,1,0:T(8,128)} copy(f32[32,64,512]{1,0,2:T(8,128)} %add_bitcast_fusion.2) | data formatting | bytes 8388608 | tf_op jit(solution)/shard_map/while/body/eval_jaxpr/add | solution.py:96
  217.2 4.9 %subtract_bitcast_fusion.2 = f32[32,64,512]{1,0,2:T(8,128)} fusion(f32[512,32,64]{2,1,0:T(8,128)S(1)} %fusion.86, bf16[64,4,512]{0,1,2:T(4,128)(2,1)S(1)} %copy-done.7, bf16[1,32,4,1024]{1,2,3,0:T(4,128)(2,1)S(1)} %copy.57), kind=kOutput, calls=%fused_computation.2.clone.1 | convolution fusion | flops 9437184 | bytes 8912896 | tf_op jit(solution)/shard_map/while/body/eval_jaxpr/csf,rsf->crf/dot_general | solution.py:101
  222.2 6.9 %copy.58 = f32[32,64,512]{2,1,0:T(8,128)} copy(f32[32,64,512]{1,0,2:T(8,128)} %subtract_bitcast_fusion.2) | data formatting | bytes 8388608 | tf_op jit(solution)/shard_map/while/body/eval_jaxpr/sub | solution.py:99
  229.1 5.8 %fusion.88 = bf16[2048,512]{1,0:T(8,128)(2,1)S(1)} fusion(bf16[1024,512]{1,0:T(8,128)(2,1)S(1)} %copy-done.2, f32[2048,512]{1,0:T(8,128)} %bitcast.74, f32[2048,512]{1,0:T(8,128)} %bitcast.73), kind=kOutput, calls=%fused_computation.6.clone.1 | convolution fusion | flops 2154823680 | bytes 11534336 | tf_op jit(solution)/shard_map/while/body/eval_jaxpr/dot_general | solution.py:103
  245.0 6.9 %copy.59 = f32[32,64,512]{2,1,0:T(8,128)} copy(f32[32,64,512]{1,0,2:T(8,128)} %add_bitcast_fusion.2) | data formatting | bytes 8388608 | tf_op jit(solution)/shard_map/while/body/eval_jaxpr/add | solution.py:96
  253.2 4.9 %subtract_bitcast_fusion.2 = f32[32,64,512]{1,0,2:T(8,128)} fusion(f32[512,32,64]{2,1,0:T(8,128)S(1)} %fusion.86, bf16[64,4,512]{0,1,2:T(4,128)(2,1)S(1)} %copy-done.7, bf16[1,32,4,1024]{1,2,3,0:T(4,128)(2,1)S(1)} %copy.57), kind=kOutput, calls=%fused_computation.2.clone.1 | convolution fusion | flops 9437184 | bytes 8912896 | tf_op jit(solution)/shard_map/while/body/eval_jaxpr/csf,rsf->crf/dot_general | solution.py:101
  258.1 6.9 %copy.58 = f32[32,64,512]{2,1,0:T(8,128)} copy(f32[32,64,512]{1,0,2:T(8,128)} %subtract_bitcast_fusion.2) | data formatting | bytes 8388608 | tf_op jit(solution)/shard_map/while/body/eval_jaxpr/sub | solution.py:99
  265.1 5.8 %fusion.88 = bf16[2048,512]{1,0:T(8,128)(2,1)S(1)} fusion(bf16[1024,512]{1,0:T(8,128)(2,1)S(1)} %copy-done.2, f32[2048,512]{1,0:T(8,128)} %bitcast.74, f32[2048,512]{1,0:T(8,128)} %bitcast.73), kind=kOutput, calls=%fused_computation.6.clone.1 | convolution fusion | flops 2154823680 | bytes 11534336 | tf_op jit(solution)/shard_map/while/body/eval_jaxpr/dot_general | solution.py:103
  276.0 4.9 %add_bitcast_fusion.2 = f32[32,64,512]{1,0,2:T(8,128)} fusion(f32[512,32,64]{2,1,0:T(8,128)S(1)} %fusion.87, bf16[64,4,512]{0,1,2:T(4,128)(2,1)S(1)} %copy-done.6, bf16[1,32,4,1024]{1,2,3,0:T(4,128)(2,1)S(1)} %copy.57), kind=kOutput, calls=%fused_computation.3.clone.1 | convolution fusion | flops 9437184 | bytes 8912896 | tf_op jit(solution)/shard_map/while/body/eval_jaxpr/csf,rsf->crf/dot_general | solution.py:98
  280.9 6.9 %copy.59 = f32[32,64,512]{2,1,0:T(8,128)} copy(f32[32,64,512]{1,0,2:T(8,128)} %add_bitcast_fusion.2) | data formatting | bytes 8388608 | tf_op jit(solution)/shard_map/while/body/eval_jaxpr/add | solution.py:96
  289.1 4.9 %subtract_bitcast_fusion.2 = f32[32,64,512]{1,0,2:T(8,128)} fusion(f32[512,32,64]{2,1,0:T(8,128)S(1)} %fusion.86, bf16[64,4,512]{0,1,2:T(4,128)(2,1)S(1)} %copy-done.7, bf16[1,32,4,1024]{1,2,3,0:T(4,128)(2,1)S(1)} %copy.57), kind=kOutput, calls=%fused_computation.2.clone.1 | convolution fusion | flops 9437184 | bytes 8912896 | tf_op jit(solution)/shard_map/while/body/eval_jaxpr/csf,rsf->crf/dot_general | solution.py:101
  294.1 6.9 %copy.58 = f32[32,64,512]{2,1,0:T(8,128)} copy(f32[32,64,512]{1,0,2:T(8,128)} %subtract_bitcast_fusion.2) | data formatting | bytes 8388608 | tf_op jit(solution)/shard_map/while/body/eval_jaxpr/sub | solution.py:99
  301.0 5.8 %fusion.88 = bf16[2048,512]{1,0:T(8,128)(2,1)S(1)} fusion(bf16[1024,512]{1,0:T(8,128)(2,1)S(1)} %copy-done.2, f32[2048,512]{1,0:T(8,128)} %bitcast.74, f32[2048,512]{1,0:T(8,128)} %bitcast.73), kind=kOutput, calls=%fused_computation.6.clone.1 | convolution fusion | flops 2154823680 | bytes 11534336 | tf_op jit(solution)/shard_map/while/body/eval_jaxpr/dot_general | solution.py:103
  (126 shorter events, 58.7 us)
Async XLA Ops:
  6.5 151.9 %all-gather.3.cloned.1.call-start = ((), (), s32[]{:S(2)}) async-start(), calls=%async_computation | async-start | bytes 4210688 | tf_op jit(solution)/shard_map/all_gather | solution.py:80
  36.3 7.6 %copy-start.11 = (s32[64]{0:T(128)S(1)}, s32[64]{0:T(128)}, u32[]{:S(2)}) copy-start(s32[64]{0:T(128)} %param.11) | copy-start | bytes 772
  38.5 124.7 %collective-permute-start = (bf16[16,4096]{1,0:T(8,128)(2,1)S(1)}, bf16[16,4096]{1,0:T(8,128)(2,1)S(1)}, u32[]{:S(2)}, u32[]{:S(2)}) collective-permute-start(bf16[16,4096]{1,0:T(8,128)(2,1)S(1)} %slice.41), channel_id=1, source_target_pairs={{0,1},{1,2},{2,3},{3,4},{4,5},{5,6},{6,7},{7,8},{8,9},{9,10},{10,1... | collective-permute-start | bytes 393224 | tf_op jit(solution)/shard_map/ppermute | solution.py:20
  42.6 120.6 %collective-permute-start.1 = (bf16[16,4096]{1,0:T(8,128)(2,1)S(1)}, bf16[16,4096]{1,0:T(8,128)(2,1)S(1)}, u32[]{:S(2)}, u32[]{:S(2)}) collective-permute-start(bf16[16,4096]{1,0:T(8,128)(2,1)S(1)} %slice.43), channel_id=1, source_target_pairs={{1,0},{2,1},{3,2},{4,3},{5,4},{6,5},{7,6},{8,7},{9,8},{10,9},{11,1... | collective-permute-start | bytes 393224 | tf_op jit(solution)/shard_map/ppermute | solution.py:23
  133.2 2.9 copy-start.10
  133.2 2.9 copy-start.9
  133.2 3.0 copy-start.8
  166.8 1.3 copy-start.6
  173.1 6.9 %copy-start.4 = (bf16[64,4,512]{0,1,2:T(4,128)(2,1)S(1)}, bf16[64,4,512]{0,1,2:T(4,128)(2,1)}, u32[]{:S(2)}) copy-start(bf16[64,4,512]{0,1,2:T(4,128)(2,1)} %get-tuple-element.174) | copy-start | bytes 786436 | tf_op jit(solution)/shard_map/while
  186.2 6.9 %copy-start.2 = (bf16[1024,512]{1,0:T(8,128)(2,1)S(1)}, bf16[1024,512]{1,0:T(8,128)(2,1)}, u32[]{:S(2)}) copy-start(bf16[1024,512]{1,0:T(8,128)(2,1)} %get-tuple-element.163) | copy-start | bytes 3145732 | tf_op jit(solution)/shard_map/while
  199.0 1.6 copy-start.1
  199.0 1.8 copy-start.5
  209.0 6.9 %copy-start.4 = (bf16[64,4,512]{0,1,2:T(4,128)(2,1)S(1)}, bf16[64,4,512]{0,1,2:T(4,128)(2,1)}, u32[]{:S(2)}) copy-start(bf16[64,4,512]{0,1,2:T(4,128)(2,1)} %get-tuple-element.174) | copy-start | bytes 786436 | tf_op jit(solution)/shard_map/while
  222.2 6.9 %copy-start.2 = (bf16[1024,512]{1,0:T(8,128)(2,1)S(1)}, bf16[1024,512]{1,0:T(8,128)(2,1)}, u32[]{:S(2)}) copy-start(bf16[1024,512]{1,0:T(8,128)(2,1)} %get-tuple-element.163) | copy-start | bytes 3145732 | tf_op jit(solution)/shard_map/while
  234.9 1.6 copy-start.1
  234.9 1.8 copy-start.5
  245.0 6.9 %copy-start.4 = (bf16[64,4,512]{0,1,2:T(4,128)(2,1)S(1)}, bf16[64,4,512]{0,1,2:T(4,128)(2,1)}, u32[]{:S(2)}) copy-start(bf16[64,4,512]{0,1,2:T(4,128)(2,1)} %get-tuple-element.174) | copy-start | bytes 786436 | tf_op jit(solution)/shard_map/while
  258.1 6.9 %copy-start.2 = (bf16[1024,512]{1,0:T(8,128)(2,1)S(1)}, bf16[1024,512]{1,0:T(8,128)(2,1)}, u32[]{:S(2)}) copy-start(bf16[1024,512]{1,0:T(8,128)(2,1)} %get-tuple-element.163) | copy-start | bytes 3145732 | tf_op jit(solution)/shard_map/while
  270.9 1.6 copy-start.1
  270.9 1.8 copy-start.5
  280.9 6.9 %copy-start.4 = (bf16[64,4,512]{0,1,2:T(4,128)(2,1)S(1)}, bf16[64,4,512]{0,1,2:T(4,128)(2,1)}, u32[]{:S(2)}) copy-start(bf16[64,4,512]{0,1,2:T(4,128)(2,1)} %get-tuple-element.174) | copy-start | bytes 786436 | tf_op jit(solution)/shard_map/while
  294.1 6.9 %copy-start.2 = (bf16[1024,512]{1,0:T(8,128)(2,1)S(1)}, bf16[1024,512]{1,0:T(8,128)(2,1)}, u32[]{:S(2)}) copy-start(bf16[1024,512]{1,0:T(8,128)(2,1)} %get-tuple-element.163) | copy-start | bytes 3145732 | tf_op jit(solution)/shard_map/while
  306.8 1.6 copy-start.1
  306.8 1.8 copy-start.5
  (12 other events, 14.3 us)
Sparse Core Ops, SparseCore 0:
  38.4 119.9 all-gather.2
where the time goes:
time: 316 us
  blocking collectives  88.9 us (28%)
  matrix products  80.2 us (25%)
  local copies, waits for them, and re-layouts  79.5 us (25%)
  other arithmetic  22.8 us (7%)
  between operations  21.9 us (7%)
  waiting for transfers between devices  16.6 us (5%)
  starting transfers between devices  5.32 us (2%)
    psum x1, blocking collectives, per_device(): references = lax.psum(selected, ('fibre', 'chan')).astype(jnp.bfloat16)  88.9 us
    add x4, local copies, waits for them, and re-layouts, correlate(): jnp.einsum('csf,rsf->crf', a_re, ref_re, preferred_element_type=jnp.float32)  27.7 us
    sub x4, local copies, waits for them, and re-layouts, correlate(): jnp.einsum('csf,rsf->crf', a_im, ref_re, preferred_element_type=jnp.float32)  27.7 us
    dot_general x4, matrix products, correlate(): jnp.dot(cross.reshape(group * REFS, SEG), kernel, preferred_element_type=...  23.2 us
    another operation x3, other arithmetic  20.4 us
    dot_general x4, matrix products, correlate(): jnp.einsum('csf,rsf->crf', a_re, ref_im, preferred_element_type=jnp.float32)  19.8 us
    dot_general x4, matrix products, correlate(): jnp.einsum('csf,rsf->crf', a_im, ref_im, preferred_element_type=jnp.float32)  19.8 us
    all_gather x1, waiting for transfers between devices, per_device(): piece = lax.all_gather(exported, ('fibre', 'chan'), axis=0, tiled=True)  16.6 us
  transfers between devices with their start and end apart: 3, of which 1 were waited for; matrix products, arithmetic and copies ran while one was open for 4% of the time, Pallas kernels for 0%

commit v1 on v0

--- a/solution.py
+++ b/solution.py
@@ -62,7 +62,9 @@
     columns = jnp.arange(local_ch, dtype=jnp.int32)
     pick = (ref_ids[:, None] - block_base == columns[None, :]).astype(jnp.bfloat16)
     selected = jnp.dot(pick, flat, preferred_element_type=jnp.float32)
-    references = lax.psum(selected, ("fibre", "chan")).astype(jnp.bfloat16)
+    references = jax.lax.psum(jax.lax.psum(selected, axis_name="fibre"), axis_name="chan").astype(
+        jnp.bfloat16
+    )
     extended = with_halo(flat, (("chan", 0),), HALO)
     ext_rows = local_ch + 2 * HALO
     position = near_ids - (block_base - HALO)

time: 316 us -> 928 us (2.94)
  the two profiles are of different devices: /device:TPU:1 before, /device:TPU:0 now
where the time goes in v1:
time: 928 us
  blocking collectives  696 us (75%)
  matrix products  81.2 us (9%)
  local copies, waits for them, and re-layouts  79.5 us (9%)
  between operations  23.4 us (3%)
  other arithmetic  22.8 us (2%)
  waiting for transfers between devices  21.4 us (2%)
    psum x1, blocking collectives, per_device(): jax.lax.psum(jax.lax.psum(selected, axis_name='fibre'), axis_name='chan')  696 us
    add x4, local copies, waits for them, and re-layouts, correlate(): jnp.einsum('csf,rsf->crf', a_re, ref_re, preferred_element_type=jnp.float32)  27.7 us
    sub x4, local copies, waits for them, and re-layouts, correlate(): jnp.einsum('csf,rsf->crf', a_im, ref_re, preferred_element_type=jnp.float32)  27.7 us
    dot_general x4, matrix products, correlate(): jnp.dot(cross.reshape(group * REFS, SEG), kernel, preferred_element_type=...  23.2 us
    psum x1, waiting for transfers between devices, per_device(): jax.lax.psum(selected, axis_name='fibre')  21.4 us
    another operation x3, other arithmetic  20.4 us
    dot_general x4, matrix products, correlate(): jnp.einsum('csf,rsf->crf', a_re, ref_im, preferred_element_type=jnp.float32)  19.8 us
    dot_general x4, matrix products, correlate(): jnp.einsum('csf,rsf->crf', a_im, ref_im, preferred_element_type=jnp.float32)  19.8 us
  transfers between devices with their start and end apart: 4, of which 1 were waited for; matrix products, arithmetic and copies ran while one was open for 2% of the time, Pallas kernels for 0%

profile of v1, /device:TPU:0, one launch (start us, length us, event | category | flops | bytes accessed | tf_op | source)
XLA Modules:
  0.0 927.5 jit_solution(11350927454836523799)
XLA Ops:
  13.9 8.0 negate_convert_fusion
  27.6 7.9 multiply_convert_fusion
  49.8 21.4 %all-reduce.3.cloned.1.call-done = f32[64,4096]{1,0:T(8,128)} async-done(((f32[64,4096]{1,0:T(8,128)}), f32[64,4096]{1,0:T(8,128)}) %all-reduce.3.cloned.1.call-update) | async-done | bytes 1048592 | tf_op jit(solution)/shard_map/psum | solution.py:65
  71.2 695.8 %all-reduce.4 = bf16[64,4096]{1,0:T(8,128)(2,1)S(1)} all-reduce(f32[64,4096]{1,0:T(8,128)} %all-reduce.3.cloned.1.call-done), channel_id=1, replica_groups=mesh['fibre'=2,'chan'=128] {'chan'}, use_global_device_ids=true, to_apply=%region_5.6 | all-reduce | flops 262144 | bytes 1572864 | tf_op jit(solution)/shard_map/psum | solution.py:65
  776.2 143.8 %while.11 = (s32[]{:T(128)}, bf16[4,32,64,512]{3,2,1,0:T(8,128)(2,1)}, bf16[4,32,4,1024]{3,2,1,0:T(4,128)(2,1)S(1)}, bf16[64,4,512]{0,1,2:T(4,128)(2,1)S(1)}, bf...) while((s32[]{:T(128)}, ...), condition=%wide.region_7.8_spmd, body=%wide.region_6.7_spmd.sunk | while | flops 2190475264 | bytes 77595424 | solution.py:108
  779.5 4.9 add_bitcast_fusion.2
  784.4 6.9 copy.59
  792.7 4.9 subtract_bitcast_fusion.2
  797.6 6.9 copy.58
  804.5 5.8 fusion.88
  815.4 4.9 add_bitcast_fusion.2
  820.4 6.9 copy.59
  828.6 4.9 subtract_bitcast_fusion.2
  833.6 6.9 copy.58
  840.5 5.8 fusion.88
  851.4 4.9 add_bitcast_fusion.2
  856.3 6.9 copy.59
  864.6 4.9 subtract_bitcast_fusion.2
  869.5 6.9 copy.58
  876.4 5.8 fusion.88
  892.3 6.9 copy.59
  900.5 4.9 subtract_bitcast_fusion.2
  905.5 6.9 copy.58
  912.4 5.8 fusion.88
  (129 shorter events, 57.5 us)
Async XLA Ops:
  7.4 63.8 %all-reduce.3.cloned.1.call-start = ((), (), s32[]{:S(2)}) async-start(), calls=%async_computation | async-start | bytes 2097152 | tf_op jit(solution)/shard_map/psum | solution.py:65
  37.9 6.1 copy-start.10
  37.9 6.1 copy-start.9
  37.9 6.3 copy-start.8
  39.3 730.6 %all-gather.3.cloned.1.call-start = ((), (), s32[]{:S(2)}) async-start(), calls=%async_computation.1 | async-start | bytes 4210688 | tf_op jit(solution)/shard_map/all_gather | solution.py:82
  40.8 733.8 %collective-permute-start = (bf16[16,4096]{1,0:T(8,128)(2,1)S(1)}, bf16[16,4096]{1,0:T(8,128)(2,1)S(1)}, u32[]{:S(2)}, u32[]{:S(2)}) collective-permute-start(bf16[16,4096]{1,0:T(8,128)(2,1)S(1)} %slice.41), channel_id=1, source_target_pairs={{0,1},{1,2},{2,3},{3,4},{4,5},{5,6},{6,7},{7,8},{8,9},{9,10},{10,1... | collective-permute-start | bytes 393224 | tf_op jit(solution)/shard_map/ppermute | solution.py:20
  42.7 731.9 %collective-permute-start.1 = (bf16[16,4096]{1,0:T(8,128)(2,1)S(1)}, bf16[16,4096]{1,0:T(8,128)(2,1)S(1)}, u32[]{:S(2)}, u32[]{:S(2)}) collective-permute-start(bf16[16,4096]{1,0:T(8,128)(2,1)S(1)} %slice.43), channel_id=1, source_target_pairs={{1,0},{2,1},{3,2},{4,3},{5,4},{6,5},{7,6},{8,7},{9,8},{10,9},{11,1... | collective-permute-start | bytes 393224 | tf_op jit(solution)/shard_map/ppermute | solution.py:23
  784.4 6.9 copy-start.4
  797.6 6.9 copy-start.2
  810.4 1.6 copy-start.1
  810.4 1.8 copy-start.5
  814.1 1.3 copy-start.6
  820.4 6.9 copy-start.4
  833.6 6.9 copy-start.2
  846.3 1.6 copy-start.1
  846.3 1.8 copy-start.5
  856.3 6.9 copy-start.4
  869.5 6.9 copy-start.2
  882.3 1.6 copy-start.1
  882.3 1.8 copy-start.5
  892.3 6.9 copy-start.4
  905.5 6.9 copy-start.2
  918.2 1.6 copy-start.1
  918.2 1.8 copy-start.5
  (13 other events, 15.3 us)
Sparse Core Ops, SparseCore 0:
  39.4 31.7 all-reduce.2
Sparse Core Ops, SparseCore 1:
  43.5 117.2 all-gather.2
